TPU v7x, 512 devices: a whole 4x8x8 slice. The times are simulated.
512 devices in a mesh: segment: 4 (over x), chan: 16 (over y, core), dp: 8 (over z).
Axes of the slice: x: 4, y: 8, z: 8, core: 2. Of those that a mesh axis runs over, the one named last changes fastest.
Arguments:
- grad_top: bfloat16 [8, 1536, 256], P('dp', None, 'chan'), may hold values from -6 to 6
- inputs_one: bfloat16 [4, 8, 1536, 256], P('segment', 'dp', 'chan'), may hold values from -6 to 6
- conv_one: bfloat16 [4, 8, 1536, 256], P('segment', 'dp', 'chan'), may hold values from -130 to 130
- inputs_two: bfloat16 [4, 8, 1536, 256], P('segment', 'dp', 'chan'), may hold values from -6 to 6
- conv_two: bfloat16 [4, 8, 1536, 256], P('segment', 'dp', 'chan'), may hold values from -130 to 130
- proj_weight: bfloat16 [4, 2, 1536, 1536], P('segment', None, 'chan'), may hold values from -0.15625 to 0.15625
- conv_weight: bfloat16 [4, 2, 1536, 432], P('segment', None, 'chan'), may hold values from -0.3125 to 0.3125
- norm_gain: float32 [4, 2, 1536], P('segment', None, 'chan'), may hold values from 0.1 to 1.9
- norm_bias: float32 [4, 2, 1536], P('segment', None, 'chan'), may hold values from -4 to 4
Outputs:
- grad_latent: bfloat16 [4, 8, 1536, 256], P('segment', 'dp', None, 'chan')
- grad_proj: float32 [4, 2, 1536, 1536], P('segment', None, 'chan')
- grad_conv: float32 [4, 2, 1536, 432], P('segment', None, 'chan')
- grad_gain: float32 [4, 2, 1536], P('segment', None, 'chan')
- grad_bias: float32 [4, 2, 1536], P('segment', None, 'chan')
All inputs are finite; a program needn't handle non-finite values.
Results may differ from a plain program's by a relative error of at most 0.009.
Values may be sent and summed in bfloat16 or wider, within the bound.
No kernel may reach another device: no remote copies, remote signals or barrier semaphores. Data moves between devices by JAX's collectives and lax.ppermute only.
A program may use at most 64 MiB of HBM per device.

v0:
```python
import jax
import jax.numpy as jnp
from jax import lax
from jax.sharding import PartitionSpec as P

GS = 48
WW = 64
NORM_EPS = 1e-05


def passed_along(block, axis, distance):
    devices = range(lax.axis_size(axis))
    route = [(i - distance, i) for i in devices if i - distance in devices]
    return lax.ppermute(block, axis, route)


def shifted_cells(values, step_row, step_col, img_width):
    length = values.shape[2]
    margin = img_width + 1
    padded = jnp.pad(values, ((0, 0), (0, 0), (margin, margin)))
    start_at = margin + step_row * img_width + step_col
    part_view = lax.slice_in_dim(padded, start_at, start_at + length, axis=2)
    column = jnp.arange(length, dtype=jnp.int32) % img_width
    inside = (column + step_col >= 0) & (column + step_col < img_width)
    return jnp.where(inside, part_view, jnp.zeros((), values.dtype))


def norm_forward(saved_pre, gain_vec, bias_vec):
    chans, positions = saved_pre.shape
    groups_here = chans // GS
    pre = saved_pre.astype(jnp.float32).reshape(groups_here, GS, positions)
    centre = jnp.mean(pre, axis=(1, 2), keepdims=True)
    varied = jnp.mean(jnp.square(pre - centre), axis=(1, 2), keepdims=True)
    inv_std = lax.rsqrt(varied + NORM_EPS)
    normed = (pre - centre) * inv_std
    gain_grid = gain_vec.reshape(groups_here, GS, 1)
    scaled = normed * gain_grid + bias_vec.reshape(groups_here, GS, 1)
    gate_vals = jax.nn.sigmoid(scaled)
    act_bf = (scaled * gate_vals).astype(jnp.bfloat16).reshape(chans, positions)
    return (normed, scaled, gate_vals, inv_std, gain_grid, act_bf)


def conv_backward(grad_act, norm_state, saved_in, w_conv):
    normed, scaled, gate_vals, inv_std, gain_grid, act_bf = norm_state
    groups_here, _, positions = normed.shape
    chans = groups_here * GS
    grad_act = grad_act.reshape(groups_here, GS, positions)
    grad_norm = grad_act * (gate_vals * (1.0 + scaled * (1.0 - gate_vals)))
    gain_grad = jnp.sum(grad_norm * normed, axis=2).reshape(chans)
    bias_grad = jnp.sum(grad_norm, axis=2).reshape(chans)
    weighted = grad_norm * gain_grid
    first_mean = jnp.mean(weighted, axis=(1, 2), keepdims=True)
    second_mean = jnp.mean(weighted * normed, axis=(1, 2), keepdims=True)
    grad_pre = (inv_std * (weighted - first_mean - normed * second_mean)).astype(jnp.bfloat16)
    saved_grid = saved_in.reshape(groups_here, GS, positions)
    taps_w = w_conv.reshape(groups_here, GS, 9, GS)
    conv_parts = []
    back_sum = jnp.zeros((groups_here, GS, positions), jnp.float32)
    for tap_row in (-1, 0, 1):
        for tap_col in (-1, 0, 1):
            tap_at = 3 * (tap_row + 1) + tap_col + 1
            source = shifted_cells(saved_grid, tap_row, tap_col, WW)
            conv_parts.append(
                jnp.einsum("gop,gjp->goj", grad_pre, source, preferred_element_type=jnp.float32)
            )
            spread_back = jnp.einsum(
                "goj,gop->gjp",
                taps_w[:, :, tap_at, :],
                grad_pre,
                preferred_element_type=jnp.float32,
            )
            back_sum = back_sum + shifted_cells(spread_back, -tap_row, -tap_col, WW)
    conv_grad = jnp.stack(conv_parts, axis=2).reshape(chans, 9 * GS)
    branch = back_sum.reshape(chans, positions).astype(jnp.bfloat16)
    return (branch, conv_grad, gain_grad, bias_grad)


def block_sharded(grad_slab, saved_in, saved_pre, w_proj, w_conv, gain_vec, bias_vec):
    norm_state = norm_forward(saved_pre, gain_vec, bias_vec)
    act_bf = norm_state[5]
    grad_piece = lax.all_gather(grad_slab, "chan", axis=1, tiled=True)
    fresh = jnp.dot(w_proj, grad_piece, preferred_element_type=jnp.float32)
    weight_acc = lax.dot_general(
        act_bf, grad_piece, (((1,), (1,)), ((), ())), preferred_element_type=jnp.float32
    )
    branch, conv_grad, gain_grad, bias_grad = conv_backward(fresh, norm_state, saved_in, w_conv)
    returned = lax.all_to_all(branch, "chan", split_axis=1, concat_axis=0, tiled=True)
    out_slab = (grad_slab.astype(jnp.float32) + returned.astype(jnp.float32)).astype(jnp.bfloat16)
    return (out_slab, (weight_acc, conv_grad, gain_grad, bias_grad))


def take_micro(saved_all, index_at):
    return lax.dynamic_index_in_dim(saved_all[0], index_at, 0, keepdims=False)


def per_device(
    grad_top,
    inputs_one,
    conv_one,
    inputs_two,
    conv_two,
    proj_weight,
    conv_weight,
    norm_gain,
    norm_bias,
):
    segments = lax.axis_size("segment")
    segment_at = lax.axis_index("segment")
    local_mb = grad_top.shape[0]
    chans = conv_one.shape[2]
    width_all = proj_weight.shape[3]
    ticks = local_mb + segments - 1
    initial = (
        jnp.zeros(grad_top.shape[1:], jnp.bfloat16),
        jnp.zeros((1,) + grad_top.shape, jnp.bfloat16),
        jnp.zeros((2, chans, width_all), jnp.float32),
        jnp.zeros((2, chans, 9 * GS), jnp.float32),
        jnp.zeros((2, chans), jnp.float32),
        jnp.zeros((2, chans), jnp.float32),
    )

    def one_tick(tick_at, running):
        received, latent, proj_acc, conv_acc, gain_acc, bias_acc = running
        micro_at = tick_at - (segments - 1 - segment_at)
        is_valid = (micro_at >= 0) & (micro_at < local_mb)
        safe_mb = jnp.clip(micro_at, 0, local_mb - 1)
        top_grad = lax.dynamic_index_in_dim(grad_top, safe_mb, 0, keepdims=False)
        entering = jnp.where(segment_at == segments - 1, top_grad, received)
        mid_grad, grads_two = block_sharded(
            entering,
            take_micro(inputs_two, safe_mb),
            take_micro(conv_two, safe_mb),
            proj_weight[0, 1],
            conv_weight[0, 1],
            norm_gain[0, 1],
            norm_bias[0, 1],
        )
        out_grad, grads_one = block_sharded(
            mid_grad,
            take_micro(inputs_one, safe_mb),
            take_micro(conv_one, safe_mb),
            proj_weight[0, 0],
            conv_weight[0, 0],
            norm_gain[0, 0],
            norm_bias[0, 0],
        )
        weight_mask = is_valid.astype(jnp.float32)
        proj_acc = proj_acc + weight_mask * jnp.stack((grads_one[0], grads_two[0]))
        conv_acc = conv_acc + weight_mask * jnp.stack((grads_one[1], grads_two[1]))
        gain_acc = gain_acc + weight_mask * jnp.stack((grads_one[2], grads_two[2]))
        bias_acc = bias_acc + weight_mask * jnp.stack((grads_one[3], grads_two[3]))
        current = lax.dynamic_index_in_dim(latent[0], safe_mb, 0, keepdims=False)
        kept = jnp.where(is_valid, out_grad, current)
        latent = lax.dynamic_update_index_in_dim(latent, kept[None, None], safe_mb, 1)
        received = passed_along(out_grad, "segment", -1)
        return (received, latent, proj_acc, conv_acc, gain_acc, bias_acc)

    final = lax.fori_loop(0, ticks, one_tick, initial)
    latent = final[1]
    proj_sum, conv_sum, gain_sum, bias_sum = lax.psum(
        (final[2], final[3], final[4], final[5]), "dp"
    )
    return (latent, proj_sum[None], conv_sum[None], gain_sum[None], bias_sum[None])


def solution(mesh):
    return jax.shard_map(
        per_device,
        mesh=mesh,
        in_specs=(
            P("dp", None, "chan"),
            P("segment", "dp", "chan", None),
            P("segment", "dp", "chan", None),
            P("segment", "dp", "chan", None),
            P("segment", "dp", "chan", None),
            P("segment", None, "chan", None),
            P("segment", None, "chan", None),
            P("segment", None, "chan"),
            P("segment", None, "chan"),
        ),
        out_specs=(
            P("segment", "dp", None, "chan"),
            P("segment", None, "chan", None),
            P("segment", None, "chan", None),
            P("segment", None, "chan"),
            P("segment", None, "chan"),
        ),
        check_vma=False,
    )
```

profile of v0, /device:TPU:2, one launch (start us, length us, event | category | flops | bytes accessed | tf_op | source)
XLA Modules:
  0.0 469.4 jit_solution(2428649469921807830)
XLA Ops:
  7.3 1.8 copy.64
  9.6 357.8 %while.26 = (s32[]{:T(128)}, bf16[1536,16]{0,1:T(8,128)(2,1)S(1)}, bf16[1,1,1536,16]{2,3,1,0:T(8,128)(2,1)}, f32[2,96,1536]{2,1,0:T(8,128)S(1)}, f32[2,96,432]{1...) while((s32[]{:T(128)}, bf16[1536,16]{0,1:T(8,128)(2,1)S(1)}, ...), condition=%wide.region_21.22_spmd.clone, body=%wide.region_0.21_spmd.clone.sunk | while | flops 392720768 | bytes 27672152 | solution.py:158
  11.2 0.9 convert_reduce_fusion.5
  12.5 1.0 multiply_reduce_fusion.13
  14.7 19.7 %all_gather.24 = bf16[1536,256]{0,1:T(8,128)(2,1)S(1)} all-gather(bf16[1536,16]{0,1:T(8,128)(2,1)S(1)} %bitcast_select_fusion.3), channel_id=1, replica_groups=mesh['segment'=4,'chan'=16,'dp'=8] {'chan'}, dimensions={1}, use_global_device_ids=true | all-gather | bytes 835584 | tf_op jit(solution)/shard_map/while/body/eval_jaxpr/all_gather | solution.py:81
  34.4 2.0 multiply_reduce_fusion.14
  37.0 1.0 fusion.353
  40.7 4.4 all-to-all-start
  52.0 1.0 all-to-all-done
  53.2 18.4 %all_gather.25 = bf16[1536,256]{0,1:T(8,128)(2,1)S(1)} all-gather(bf16[1536,16]{0,1:T(8,128)(2,1)S(1)} %add_convert_fusion.4), channel_id=1, replica_groups=mesh['segment'=4,'chan'=16,'dp'=8] {'chan'}, dimensions={1}, use_global_device_ids=true | all-gather | bytes 835584 | tf_op jit(solution)/shard_map/while/body/eval_jaxpr/all_gather | solution.py:81
  71.6 2.0 multiply_reduce_fusion.15
  76.8 4.6 all-to-all-start.1
  81.5 0.8 fusion.369
  88.9 1.2 copy.167
  91.7 1.4 fusion.358
  93.2 3.9 collective-permute-start
  97.2 1.9 collective-permute-done
  100.8 0.9 convert_reduce_fusion.5
  102.1 1.0 multiply_reduce_fusion.13
  104.2 19.4 %all_gather.24 = bf16[1536,256]{0,1:T(8,128)(2,1)S(1)} all-gather(bf16[1536,16]{0,1:T(8,128)(2,1)S(1)} %bitcast_select_fusion.3), channel_id=1, replica_groups=mesh['segment'=4,'chan'=16,'dp'=8] {'chan'}, dimensions={1}, use_global_device_ids=true | all-gather | bytes 835584 | tf_op jit(solution)/shard_map/while/body/eval_jaxpr/all_gather | solution.py:81
  123.6 2.0 multiply_reduce_fusion.14
  126.2 1.0 fusion.353
  129.9 4.6 all-to-all-start
  141.4 1.0 all-to-all-done
  142.6 18.4 %all_gather.25 = bf16[1536,256]{0,1:T(8,128)(2,1)S(1)} all-gather(bf16[1536,16]{0,1:T(8,128)(2,1)S(1)} %add_convert_fusion.4), channel_id=1, replica_groups=mesh['segment'=4,'chan'=16,'dp'=8] {'chan'}, dimensions={1}, use_global_device_ids=true | all-gather | bytes 835584 | tf_op jit(solution)/shard_map/while/body/eval_jaxpr/all_gather | solution.py:81
  161.0 2.0 multiply_reduce_fusion.15
  166.3 4.6 all-to-all-start.1
  170.9 0.8 fusion.369
  178.3 1.2 copy.167
  181.2 1.4 fusion.358
  182.6 3.9 collective-permute-start
  186.6 1.9 collective-permute-done
  190.2 0.9 convert_reduce_fusion.5
  191.5 1.0 multiply_reduce_fusion.13
  193.7 19.4 %all_gather.24 = bf16[1536,256]{0,1:T(8,128)(2,1)S(1)} all-gather(bf16[1536,16]{0,1:T(8,128)(2,1)S(1)} %bitcast_select_fusion.3), channel_id=1, replica_groups=mesh['segment'=4,'chan'=16,'dp'=8] {'chan'}, dimensions={1}, use_global_device_ids=true | all-gather | bytes 835584 | tf_op jit(solution)/shard_map/while/body/eval_jaxpr/all_gather | solution.py:81
  213.1 2.0 multiply_reduce_fusion.14
  215.7 1.0 fusion.353
  219.4 4.6 all-to-all-start
  230.9 1.0 all-to-all-done
  232.1 18.4 %all_gather.25 = bf16[1536,256]{0,1:T(8,128)(2,1)S(1)} all-gather(bf16[1536,16]{0,1:T(8,128)(2,1)S(1)} %add_convert_fusion.4), channel_id=1, replica_groups=mesh['segment'=4,'chan'=16,'dp'=8] {'chan'}, dimensions={1}, use_global_device_ids=true | all-gather | bytes 835584 | tf_op jit(solution)/shard_map/while/body/eval_jaxpr/all_gather | solution.py:81
  250.5 2.0 multiply_reduce_fusion.15
  255.7 4.6 all-to-all-start.1
  267.8 1.2 copy.167
  270.6 1.4 fusion.358
  272.1 3.9 collective-permute-start
  276.1 1.9 collective-permute-done
  279.7 0.9 convert_reduce_fusion.5
  280.9 1.0 multiply_reduce_fusion.13
  283.1 19.4 %all_gather.24 = bf16[1536,256]{0,1:T(8,128)(2,1)S(1)} all-gather(bf16[1536,16]{0,1:T(8,128)(2,1)S(1)} %bitcast_select_fusion.3), channel_id=1, replica_groups=mesh['segment'=4,'chan'=16,'dp'=8] {'chan'}, dimensions={1}, use_global_device_ids=true | all-gather | bytes 835584 | tf_op jit(solution)/shard_map/while/body/eval_jaxpr/all_gather | solution.py:81
  302.5 2.0 multiply_reduce_fusion.14
  305.1 1.0 fusion.353
  308.8 4.6 all-to-all-start
  320.3 1.0 all-to-all-done
  321.5 18.4 %all_gather.25 = bf16[1536,256]{0,1:T(8,128)(2,1)S(1)} all-gather(bf16[1536,16]{0,1:T(8,128)(2,1)S(1)} %add_convert_fusion.4), channel_id=1, replica_groups=mesh['segment'=4,'chan'=16,'dp'=8] {'chan'}, dimensions={1}, use_global_device_ids=true | all-gather | bytes 835584 | tf_op jit(solution)/shard_map/while/body/eval_jaxpr/all_gather | solution.py:81
  339.9 2.0 multiply_reduce_fusion.15
  345.1 4.6 all-to-all-start.1
  357.2 1.2 copy.167
  360.0 1.4 fusion.358
  361.5 3.9 collective-permute-start
  365.5 1.9 collective-permute-done
  367.5 2.4 copy.65
  369.9 23.8 %all-reduce.18 = (f32[1,2,96]{2,1,0:T(2,128)}, f32[1,2,96]{2,1,0:T(2,128)}) all-reduce(f32[1,2,96]{2,1,0:T(2,128)S(1)} %bitcast.586, f32[1,2,96]{2,1,0:T(2,128)S(1)} %bitcast.587), channel_id=1, replica_groups=mesh['segment'=4,'chan'=16,'dp'=8] {'dp'}, use_global_device_ids=true, to_apply=%region_24.25 | all-reduce | flops 384 | bytes 3072 | tf_op jit(solution)/shard_map/psum | solution.py:160
  393.7 65.7 %all-reduce.22.cloned.1.call-done = (f32[1,2,96,1536]{3,2,1,0:T(8,128)}, f32[1,2,96,432]{3,2,1,0:T(8,128)}) async-done(((f32[1,2,96,1536]{3,2,1,0:T(8,128)}, f32[1,2,96,432]{3,2,1,0:T(8,128)}), (f32[1,2,96,1536]{3,2,1,0:T(8,128)}, f32[1,2,96,432]{3,2,1,0:T(8,128)})) %all-reduce.22.cloned.1.call-update) | async-done | bytes 1511440 | tf_op jit(solution)/shard_map/psum | solution.py:160
  459.4 2.4 copy.207
  (667 shorter events, 101.1 us)
Async XLA Ops:
  7.2 452.2 %all-reduce.22.cloned.1.call-start = ((), (), s32[]{:S(2)}) async-start(), calls=%async_computation.2 | async-start | bytes 3145728 | tf_op jit(solution)/shard_map/psum | solution.py:160
  9.7 29.8 %copy-start.30 = (pred[256]{0:T(512)(128)(4,1)}, pred[256]{0:T(512)(128)(4,1)S(1)}, u32[]{:S(2)}) copy-start(pred[256]{0:T(512)(128)(4,1)S(1)} %compare_and_fusion.7) | copy-start | bytes 772 | tf_op jit(solution)/shard_map/while
  9.7 29.8 %copy-start.27 = (pred[256]{0:T(512)(128)(4,1)}, pred[256]{0:T(512)(128)(4,1)S(1)}, u32[]{:S(2)}) copy-start(pred[256]{0:T(512)(128)(4,1)S(1)} %compare_and_fusion.8) | copy-start | bytes 772 | tf_op jit(solution)/shard_map/while
  38.8 6.3 %copy-start.2 = (bf16[1,1,96,256]{3,2,1,0:T(8,128)(2,1)S(1)}, bf16[1,1,96,256]{3,2,1,0:T(8,128)(2,1)}, u32[]{:S(2)}) copy-start(bf16[1,1,96,256]{3,2,1,0:T(8,128)(2,1)} %get-tuple-element.854) | copy-start | bytes 147460 | tf_op jit(solution)/shard_map/while
  39.5 9.8 %copy-start.7 = (bf16[1,1,96,256]{3,2,1,0:T(8,128)(2,1)S(1)}, bf16[1,1,96,256]{3,2,1,0:T(8,128)(2,1)}, u32[]{:S(2)}) copy-start(bf16[1,1,96,256]{3,2,1,0:T(8,128)(2,1)} %get-tuple-element.857) | copy-start | bytes 147460 | tf_op jit(solution)/shard_map/while
  39.8 9.5 %copy-start.31 = (pred[256]{0:T(512)(128)(4,1)S(1)}, pred[256]{0:T(512)(128)(4,1)}, u32[]{:S(2)}) copy-start(pred[256]{0:T(512)(128)(4,1)} %copy-done.30) | copy-start | bytes 772 | tf_op jit(solution)/shard_map/while
  39.8 9.9 %copy-start.28 = (pred[256]{0:T(512)(128)(4,1)S(1)}, pred[256]{0:T(512)(128)(4,1)}, u32[]{:S(2)}) copy-start(pred[256]{0:T(512)(128)(4,1)} %copy-done.27) | copy-start | bytes 772 | tf_op jit(solution)/shard_map/while
  40.7 12.3 %all-to-all-start = ((bf16[96,16,16]{0,2,1:T(8,128)(2,1)}), bf16[96,16,16]{0,2,1:T(8,128)(2,1)S(1)}, u32[]{:S(2)}, u32[]{:S(2)}) async-start(bf16[96,16,16]{0,2,1:T(8,128)(2,1)} %convert_element_type.430), calls=%async_computation | async-start | bytes 131072 | tf_op jit(solution)/shard_map/while/body/eval_jaxpr/all_to_all | solution.py:87
  52.0 19.6 %copy-start.22 = (f32[96]{0:T(128)S(1)}, f32[96]{0:T(128)}, u32[]{:S(2)}) copy-start(f32[96]{0:T(128)} %mul.953) | copy-start | bytes 1156 | tf_op jit(solution)/shard_map/while
  75.0 6.5 %copy-start.6 = (bf16[1,1,96,256]{3,2,1,0:T(8,128)(2,1)S(1)}, bf16[1,1,96,256]{3,2,1,0:T(8,128)(2,1)}, u32[]{:S(2)}) copy-start(bf16[1,1,96,256]{3,2,1,0:T(8,128)(2,1)} %get-tuple-element.856) | copy-start | bytes 147460 | tf_op jit(solution)/shard_map/while
  76.8 14.7 %all-to-all-start.1 = ((bf16[96,16,16]{0,2,1:T(8,128)(2,1)}), bf16[96,16,16]{0,2,1:T(8,128)(2,1)S(1)}, u32[]{:S(2)}, u32[]{:S(2)}) async-start(bf16[96,16,16]{0,2,1:T(8,128)(2,1)} %convert_element_type.431), calls=%async_computation.1 | async-start | bytes 131072 | tf_op jit(solution)/shard_map/while/body/eval_jaxpr/all_to_all | solution.py:87
  90.8 6.3 %copy-start.10 = (f32[2,96]{1,0:T(2,128)S(1)}, f32[2,96]{1,0:T(2,128)}, u32[]{:S(2)}) copy-start(f32[2,96]{1,0:T(2,128)} %get-tuple-element.824) | copy-start | bytes 2308 | tf_op jit(solution)/shard_map/while
  90.8 6.3 %copy-start.13 = (f32[2,96]{1,0:T(2,128)S(1)}, f32[2,96]{1,0:T(2,128)}, u32[]{:S(2)}) copy-start(f32[2,96]{1,0:T(2,128)} %get-tuple-element.825) | copy-start | bytes 2308 | tf_op jit(solution)/shard_map/while
  90.8 6.3 %copy-start.23 = (f32[96]{0:T(128)S(1)}, f32[96]{0:T(128)}, u32[]{:S(2)}) copy-start(f32[96]{0:T(128)} %get-tuple-element.792) | copy-start | bytes 1156 | tf_op jit(solution)/shard_map/while
  90.8 6.3 %copy-start.24 = (f32[96]{0:T(128)S(1)}, f32[96]{0:T(128)}, u32[]{:S(2)}) copy-start(f32[96]{0:T(128)} %get-tuple-element.794) | copy-start | bytes 1156 | tf_op jit(solution)/shard_map/while
  90.8 6.3 %copy-start.25 = (f32[96]{0:T(128)S(1)}, f32[96]{0:T(128)}, u32[]{:S(2)}) copy-start(f32[96]{0:T(128)} %get-tuple-element.793) | copy-start | bytes 1156 | tf_op jit(solution)/shard_map/while
  90.9 6.3 %copy-start.26 = (f32[96]{0:T(128)S(1)}, f32[96]{0:T(128)}, u32[]{:S(2)}) copy-start(f32[96]{0:T(128)} %get-tuple-element.795) | copy-start | bytes 1156 | tf_op jit(solution)/shard_map/while
  91.5 7.6 %copy-start.4 = (f32[2,96,432]{1,2,0:T(8,128)}, f32[2,96,432]{1,2,0:T(8,128)S(1)}, u32[]{:S(2)}) copy-start(f32[2,96,432]{1,2,0:T(8,128)S(1)} %fusion.378) | copy-start | bytes 995332 | tf_op jit(solution)/shard_map/while
  93.2 6.0 %collective-permute-start = (bf16[1536,16]{0,1:T(8,128)(2,1)S(1)}, bf16[1536,16]{0,1:T(8,128)(2,1)S(1)}, u32[]{:S(2)}, u32[]{:S(2)}) collective-permute-start(bf16[1536,16]{0,1:T(8,128)(2,1)S(1)} %get-tuple-element.790), channel_id=1, source_target_pairs={{128,0},{256,128},{384,256},{129,1},{257,129},{385,257},{130,2},{2... | collective-permute-start | bytes 147464 | tf_op jit(solution)/shard_map/while/body/eval_jaxpr/ppermute | solution.py:14
  99.2 29.5 %copy-start.30 = (pred[256]{0:T(512)(128)(4,1)}, pred[256]{0:T(512)(128)(4,1)S(1)}, u32[]{:S(2)}) copy-start(pred[256]{0:T(512)(128)(4,1)S(1)} %compare_and_fusion.7) | copy-start | bytes 772 | tf_op jit(solution)/shard_map/while
  99.2 29.5 %copy-start.27 = (pred[256]{0:T(512)(128)(4,1)}, pred[256]{0:T(512)(128)(4,1)S(1)}, u32[]{:S(2)}) copy-start(pred[256]{0:T(512)(128)(4,1)S(1)} %compare_and_fusion.8) | copy-start | bytes 772 | tf_op jit(solution)/shard_map/while
  128.0 6.5 %copy-start.2 = (bf16[1,1,96,256]{3,2,1,0:T(8,128)(2,1)S(1)}, bf16[1,1,96,256]{3,2,1,0:T(8,128)(2,1)}, u32[]{:S(2)}) copy-start(bf16[1,1,96,256]{3,2,1,0:T(8,128)(2,1)} %get-tuple-element.854) | copy-start | bytes 147460 | tf_op jit(solution)/shard_map/while
  128.7 10.0 %copy-start.7 = (bf16[1,1,96,256]{3,2,1,0:T(8,128)(2,1)S(1)}, bf16[1,1,96,256]{3,2,1,0:T(8,128)(2,1)}, u32[]{:S(2)}) copy-start(bf16[1,1,96,256]{3,2,1,0:T(8,128)(2,1)} %get-tuple-element.857) | copy-start | bytes 147460 | tf_op jit(solution)/shard_map/while
  129.0 9.7 %copy-start.31 = (pred[256]{0:T(512)(128)(4,1)S(1)}, pred[256]{0:T(512)(128)(4,1)}, u32[]{:S(2)}) copy-start(pred[256]{0:T(512)(128)(4,1)} %copy-done.30) | copy-start | bytes 772 | tf_op jit(solution)/shard_map/while
  129.0 10.1 %copy-start.28 = (pred[256]{0:T(512)(128)(4,1)S(1)}, pred[256]{0:T(512)(128)(4,1)}, u32[]{:S(2)}) copy-start(pred[256]{0:T(512)(128)(4,1)} %copy-done.27) | copy-start | bytes 772 | tf_op jit(solution)/shard_map/while
  129.9 12.5 %all-to-all-start = ((bf16[96,16,16]{0,2,1:T(8,128)(2,1)}), bf16[96,16,16]{0,2,1:T(8,128)(2,1)S(1)}, u32[]{:S(2)}, u32[]{:S(2)}) async-start(bf16[96,16,16]{0,2,1:T(8,128)(2,1)} %convert_element_type.430), calls=%async_computation | async-start | bytes 131072 | tf_op jit(solution)/shard_map/while/body/eval_jaxpr/all_to_all | solution.py:87
  141.4 19.6 %copy-start.22 = (f32[96]{0:T(128)S(1)}, f32[96]{0:T(128)}, u32[]{:S(2)}) copy-start(f32[96]{0:T(128)} %mul.953) | copy-start | bytes 1156 | tf_op jit(solution)/shard_map/while
  164.4 6.5 %copy-start.6 = (bf16[1,1,96,256]{3,2,1,0:T(8,128)(2,1)S(1)}, bf16[1,1,96,256]{3,2,1,0:T(8,128)(2,1)}, u32[]{:S(2)}) copy-start(bf16[1,1,96,256]{3,2,1,0:T(8,128)(2,1)} %get-tuple-element.856) | copy-start | bytes 147460 | tf_op jit(solution)/shard_map/while
  166.3 14.7 %all-to-all-start.1 = ((bf16[96,16,16]{0,2,1:T(8,128)(2,1)}), bf16[96,16,16]{0,2,1:T(8,128)(2,1)S(1)}, u32[]{:S(2)}, u32[]{:S(2)}) async-start(bf16[96,16,16]{0,2,1:T(8,128)(2,1)} %convert_element_type.431), calls=%async_computation.1 | async-start | bytes 131072 | tf_op jit(solution)/shard_map/while/body/eval_jaxpr/all_to_all | solution.py:87
  180.2 6.3 %copy-start.10 = (f32[2,96]{1,0:T(2,128)S(1)}, f32[2,96]{1,0:T(2,128)}, u32[]{:S(2)}) copy-start(f32[2,96]{1,0:T(2,128)} %get-tuple-element.824) | copy-start | bytes 2308 | tf_op jit(solution)/shard_map/while
  180.2 6.3 %copy-start.13 = (f32[2,96]{1,0:T(2,128)S(1)}, f32[2,96]{1,0:T(2,128)}, u32[]{:S(2)}) copy-start(f32[2,96]{1,0:T(2,128)} %get-tuple-element.825) | copy-start | bytes 2308 | tf_op jit(solution)/shard_map/while
  180.3 6.3 %copy-start.23 = (f32[96]{0:T(128)S(1)}, f32[96]{0:T(128)}, u32[]{:S(2)}) copy-start(f32[96]{0:T(128)} %get-tuple-element.792) | copy-start | bytes 1156 | tf_op jit(solution)/shard_map/while
  180.3 6.3 %copy-start.24 = (f32[96]{0:T(128)S(1)}, f32[96]{0:T(128)}, u32[]{:S(2)}) copy-start(f32[96]{0:T(128)} %get-tuple-element.794) | copy-start | bytes 1156 | tf_op jit(solution)/shard_map/while
  180.3 6.3 %copy-start.25 = (f32[96]{0:T(128)S(1)}, f32[96]{0:T(128)}, u32[]{:S(2)}) copy-start(f32[96]{0:T(128)} %get-tuple-element.793) | copy-start | bytes 1156 | tf_op jit(solution)/shard_map/while
  181.0 7.6 %copy-start.4 = (f32[2,96,432]{1,2,0:T(8,128)}, f32[2,96,432]{1,2,0:T(8,128)S(1)}, u32[]{:S(2)}) copy-start(f32[2,96,432]{1,2,0:T(8,128)S(1)} %fusion.378) | copy-start | bytes 995332 | tf_op jit(solution)/shard_map/while
  182.6 6.0 %collective-permute-start = (bf16[1536,16]{0,1:T(8,128)(2,1)S(1)}, bf16[1536,16]{0,1:T(8,128)(2,1)S(1)}, u32[]{:S(2)}, u32[]{:S(2)}) collective-permute-start(bf16[1536,16]{0,1:T(8,128)(2,1)S(1)} %get-tuple-element.790), channel_id=1, source_target_pairs={{128,0},{256,128},{384,256},{129,1},{257,129},{385,257},{130,2},{2... | collective-permute-start | bytes 147464 | tf_op jit(solution)/shard_map/while/body/eval_jaxpr/ppermute | solution.py:14
  188.6 29.5 %copy-start.30 = (pred[256]{0:T(512)(128)(4,1)}, pred[256]{0:T(512)(128)(4,1)S(1)}, u32[]{:S(2)}) copy-start(pred[256]{0:T(512)(128)(4,1)S(1)} %compare_and_fusion.7) | copy-start | bytes 772 | tf_op jit(solution)/shard_map/while
  188.7 29.5 %copy-start.27 = (pred[256]{0:T(512)(128)(4,1)}, pred[256]{0:T(512)(128)(4,1)S(1)}, u32[]{:S(2)}) copy-start(pred[256]{0:T(512)(128)(4,1)S(1)} %compare_and_fusion.8) | copy-start | bytes 772 | tf_op jit(solution)/shard_map/while
  217.5 6.5 %copy-start.2 = (bf16[1,1,96,256]{3,2,1,0:T(8,128)(2,1)S(1)}, bf16[1,1,96,256]{3,2,1,0:T(8,128)(2,1)}, u32[]{:S(2)}) copy-start(bf16[1,1,96,256]{3,2,1,0:T(8,128)(2,1)} %get-tuple-element.854) | copy-start | bytes 147460 | tf_op jit(solution)/shard_map/while
  218.2 10.0 %copy-start.7 = (bf16[1,1,96,256]{3,2,1,0:T(8,128)(2,1)S(1)}, bf16[1,1,96,256]{3,2,1,0:T(8,128)(2,1)}, u32[]{:S(2)}) copy-start(bf16[1,1,96,256]{3,2,1,0:T(8,128)(2,1)} %get-tuple-element.857) | copy-start | bytes 147460 | tf_op jit(solution)/shard_map/while
  218.5 9.7 %copy-start.31 = (pred[256]{0:T(512)(128)(4,1)S(1)}, pred[256]{0:T(512)(128)(4,1)}, u32[]{:S(2)}) copy-start(pred[256]{0:T(512)(128)(4,1)} %copy-done.30) | copy-start | bytes 772 | tf_op jit(solution)/shard_map/while
  218.5 10.1 %copy-start.28 = (pred[256]{0:T(512)(128)(4,1)S(1)}, pred[256]{0:T(512)(128)(4,1)}, u32[]{:S(2)}) copy-start(pred[256]{0:T(512)(128)(4,1)} %copy-done.27) | copy-start | bytes 772 | tf_op jit(solution)/shard_map/while
  219.4 12.5 %all-to-all-start = ((bf16[96,16,16]{0,2,1:T(8,128)(2,1)}), bf16[96,16,16]{0,2,1:T(8,128)(2,1)S(1)}, u32[]{:S(2)}, u32[]{:S(2)}) async-start(bf16[96,16,16]{0,2,1:T(8,128)(2,1)} %convert_element_type.430), calls=%async_computation | async-start | bytes 131072 | tf_op jit(solution)/shard_map/while/body/eval_jaxpr/all_to_all | solution.py:87
  230.9 19.6 %copy-start.22 = (f32[96]{0:T(128)S(1)}, f32[96]{0:T(128)}, u32[]{:S(2)}) copy-start(f32[96]{0:T(128)} %mul.953) | copy-start | bytes 1156 | tf_op jit(solution)/shard_map/while
  253.8 6.5 %copy-start.6 = (bf16[1,1,96,256]{3,2,1,0:T(8,128)(2,1)S(1)}, bf16[1,1,96,256]{3,2,1,0:T(8,128)(2,1)}, u32[]{:S(2)}) copy-start(bf16[1,1,96,256]{3,2,1,0:T(8,128)(2,1)} %get-tuple-element.856) | copy-start | bytes 147460 | tf_op jit(solution)/shard_map/while
  255.7 14.7 %all-to-all-start.1 = ((bf16[96,16,16]{0,2,1:T(8,128)(2,1)}), bf16[96,16,16]{0,2,1:T(8,128)(2,1)S(1)}, u32[]{:S(2)}, u32[]{:S(2)}) async-start(bf16[96,16,16]{0,2,1:T(8,128)(2,1)} %convert_element_type.431), calls=%async_computation.1 | async-start | bytes 131072 | tf_op jit(solution)/shard_map/while/body/eval_jaxpr/all_to_all | solution.py:87
  269.7 6.3 %copy-start.10 = (f32[2,96]{1,0:T(2,128)S(1)}, f32[2,96]{1,0:T(2,128)}, u32[]{:S(2)}) copy-start(f32[2,96]{1,0:T(2,128)} %get-tuple-element.824) | copy-start | bytes 2308 | tf_op jit(solution)/shard_map/while
  269.7 6.3 %copy-start.13 = (f32[2,96]{1,0:T(2,128)S(1)}, f32[2,96]{1,0:T(2,128)}, u32[]{:S(2)}) copy-start(f32[2,96]{1,0:T(2,128)} %get-tuple-element.825) | copy-start | bytes 2308 | tf_op jit(solution)/shard_map/while
  270.4 7.6 %copy-start.4 = (f32[2,96,432]{1,2,0:T(8,128)}, f32[2,96,432]{1,2,0:T(8,128)S(1)}, u32[]{:S(2)}) copy-start(f32[2,96,432]{1,2,0:T(8,128)S(1)} %fusion.378) | copy-start | bytes 995332 | tf_op jit(solution)/shard_map/while
  272.1 6.0 %collective-permute-start = (bf16[1536,16]{0,1:T(8,128)(2,1)S(1)}, bf16[1536,16]{0,1:T(8,128)(2,1)S(1)}, u32[]{:S(2)}, u32[]{:S(2)}) collective-permute-start(bf16[1536,16]{0,1:T(8,128)(2,1)S(1)} %get-tuple-element.790), channel_id=1, source_target_pairs={{128,0},{256,128},{384,256},{129,1},{257,129},{385,257},{130,2},{2... | collective-permute-start | bytes 147464 | tf_op jit(solution)/shard_map/while/body/eval_jaxpr/ppermute | solution.py:14
  278.1 29.5 %copy-start.30 = (pred[256]{0:T(512)(128)(4,1)}, pred[256]{0:T(512)(128)(4,1)S(1)}, u32[]{:S(2)}) copy-start(pred[256]{0:T(512)(128)(4,1)S(1)} %compare_and_fusion.7) | copy-start | bytes 772 | tf_op jit(solution)/shard_map/while
  278.1 29.5 %copy-start.27 = (pred[256]{0:T(512)(128)(4,1)}, pred[256]{0:T(512)(128)(4,1)S(1)}, u32[]{:S(2)}) copy-start(pred[256]{0:T(512)(128)(4,1)S(1)} %compare_and_fusion.8) | copy-start | bytes 772 | tf_op jit(solution)/shard_map/while
  306.9 6.5 %copy-start.2 = (bf16[1,1,96,256]{3,2,1,0:T(8,128)(2,1)S(1)}, bf16[1,1,96,256]{3,2,1,0:T(8,128)(2,1)}, u32[]{:S(2)}) copy-start(bf16[1,1,96,256]{3,2,1,0:T(8,128)(2,1)} %get-tuple-element.854) | copy-start | bytes 147460 | tf_op jit(solution)/shard_map/while
  307.6 10.0 %copy-start.7 = (bf16[1,1,96,256]{3,2,1,0:T(8,128)(2,1)S(1)}, bf16[1,1,96,256]{3,2,1,0:T(8,128)(2,1)}, u32[]{:S(2)}) copy-start(bf16[1,1,96,256]{3,2,1,0:T(8,128)(2,1)} %get-tuple-element.857) | copy-start | bytes 147460 | tf_op jit(solution)/shard_map/while
  307.9 9.7 %copy-start.31 = (pred[256]{0:T(512)(128)(4,1)S(1)}, pred[256]{0:T(512)(128)(4,1)}, u32[]{:S(2)}) copy-start(pred[256]{0:T(512)(128)(4,1)} %copy-done.30) | copy-start | bytes 772 | tf_op jit(solution)/shard_map/while
  307.9 10.1 %copy-start.28 = (pred[256]{0:T(512)(128)(4,1)S(1)}, pred[256]{0:T(512)(128)(4,1)}, u32[]{:S(2)}) copy-start(pred[256]{0:T(512)(128)(4,1)} %copy-done.27) | copy-start | bytes 772 | tf_op jit(solution)/shard_map/while
  308.8 12.5 %all-to-all-start = ((bf16[96,16,16]{0,2,1:T(8,128)(2,1)}), bf16[96,16,16]{0,2,1:T(8,128)(2,1)S(1)}, u32[]{:S(2)}, u32[]{:S(2)}) async-start(bf16[96,16,16]{0,2,1:T(8,128)(2,1)} %convert_element_type.430), calls=%async_computation | async-start | bytes 131072 | tf_op jit(solution)/shard_map/while/body/eval_jaxpr/all_to_all | solution.py:87
  320.3 19.6 %copy-start.22 = (f32[96]{0:T(128)S(1)}, f32[96]{0:T(128)}, u32[]{:S(2)}) copy-start(f32[96]{0:T(128)} %mul.953) | copy-start | bytes 1156 | tf_op jit(solution)/shard_map/while
  343.3 6.5 %copy-start.6 = (bf16[1,1,96,256]{3,2,1,0:T(8,128)(2,1)S(1)}, bf16[1,1,96,256]{3,2,1,0:T(8,128)(2,1)}, u32[]{:S(2)}) copy-start(bf16[1,1,96,256]{3,2,1,0:T(8,128)(2,1)} %get-tuple-element.856) | copy-start | bytes 147460 | tf_op jit(solution)/shard_map/while
  345.1 14.7 %all-to-all-start.1 = ((bf16[96,16,16]{0,2,1:T(8,128)(2,1)}), bf16[96,16,16]{0,2,1:T(8,128)(2,1)S(1)}, u32[]{:S(2)}, u32[]{:S(2)}) async-start(bf16[96,16,16]{0,2,1:T(8,128)(2,1)} %convert_element_type.431), calls=%async_computation.1 | async-start | bytes 131072 | tf_op jit(solution)/shard_map/while/body/eval_jaxpr/all_to_all | solution.py:87
  359.1 6.3 %copy-start.10 = (f32[2,96]{1,0:T(2,128)S(1)}, f32[2,96]{1,0:T(2,128)}, u32[]{:S(2)}) copy-start(f32[2,96]{1,0:T(2,128)} %get-tuple-element.824) | copy-start | bytes 2308 | tf_op jit(solution)/shard_map/while
  359.1 6.3 %copy-start.13 = (f32[2,96]{1,0:T(2,128)S(1)}, f32[2,96]{1,0:T(2,128)}, u32[]{:S(2)}) copy-start(f32[2,96]{1,0:T(2,128)} %get-tuple-element.825) | copy-start | bytes 2308 | tf_op jit(solution)/shard_map/while
  359.8 7.6 %copy-start.4 = (f32[2,96,432]{1,2,0:T(8,128)}, f32[2,96,432]{1,2,0:T(8,128)S(1)}, u32[]{:S(2)}) copy-start(f32[2,96,432]{1,2,0:T(8,128)S(1)} %fusion.378) | copy-start | bytes 995332 | tf_op jit(solution)/shard_map/while
  361.5 6.0 %collective-permute-start = (bf16[1536,16]{0,1:T(8,128)(2,1)S(1)}, bf16[1536,16]{0,1:T(8,128)(2,1)S(1)}, u32[]{:S(2)}, u32[]{:S(2)}) collective-permute-start(bf16[1536,16]{0,1:T(8,128)(2,1)S(1)} %get-tuple-element.790), channel_id=1, source_target_pairs={{128,0},{256,128},{384,256},{129,1},{257,129},{385,257},{130,2},{2... | collective-permute-start | bytes 147464 | tf_op jit(solution)/shard_map/while/body/eval_jaxpr/ppermute | solution.py:14
  (69 other events, 161.8 us)
Sparse Core Ops, SparseCore 0:
  370.0 89.2 all-reduce.21
where the time goes:
time: 472 us; the launch traced here: 469 us
  blocking collectives  175 us (37%)
  waiting for transfers between devices  77.5 us (16%)
  matrix products  66.1 us (14%)
  local copies, waits for them, and re-layouts  56 us (12%)
  starting transfers between devices  52.6 us (11%)
  other arithmetic  25.2 us (5%)
  between operations  14.1 us (3%)
    all_gather x8, blocking collectives, block_sharded(): grad_piece = lax.all_gather(grad_slab, 'chan', axis=1, tiled=True)  152 us
    psum x1, waiting for transfers between devices, per_device(): lax.psum((final[2], final[3], final[4], final[5]), 'dp')  65.7 us
    dot_general x72, matrix products, conv_backward(): jnp.einsum('gop,gjp->goj', grad_pre, source, preferred_element_type=jnp.f...  36.9 us
    all_to_all x8, starting transfers between devices, block_sharded(): lax.all_to_all(branch, 'chan', split_axis=1, concat_axis=0, tiled=True)  36.9 us
    psum x1, blocking collectives, per_device(): lax.psum((final[2], final[3], final[4], final[5]), 'dp')  23.8 us
    dot_general x8, matrix products, block_sharded(): fresh = jnp.dot(w_proj, grad_piece, preferred_element_type=jnp.float32)  16 us
    ppermute x4, starting transfers between devices, passed_along(): return lax.ppermute(block, axis, route)  15.7 us
    dot_general x72, matrix products, conv_backward(): jnp.einsum('goj,gop->gjp', taps_w[:, :, tap_at, :], grad_pre, preferred_e...  10.6 us
  transfers between devices with their start and end apart: 13, of which 9 were waited for; matrix products, arithmetic and copies ran while one was open for 13% of the time, Pallas kernels for 0%

commit v1 on v0

--- a/solution.py
+++ b/solution.py
@@ -1,3 +1,4 @@
+import functools
 import jax
 import jax.numpy as jnp
 from jax import lax
@@ -6,6 +7,23 @@
 GS = 48
 WW = 64
 NORM_EPS = 1e-05
+
+
+def _direct_map(sheet, chip_axis, dim_at):
+    p_count = jax.lax.axis_size(chip_axis)
+    part_next = sorted(((w, (w + 1) % p_count) for w in range(p_count)))
+    piece_next = sheet
+    all_rows = [piece_next]
+    for dev_j in range(1, p_count):
+        piece_next = jax.lax.ppermute(piece_next, chip_axis, part_next)
+        all_rows.insert(0, piece_next)
+    small = jnp.concatenate(all_rows, axis=dim_at)
+    return jnp.roll(
+        small, shift=(jax.lax.axis_index(chip_axis) + 1) * sheet.shape[dim_at], axis=dim_at
+    )
+
+
+obtain_the_cells = functools.partial(_direct_map, chip_axis="chan", dim_at=1)
 
 
 def passed_along(block, axis, distance):
@@ -78,7 +96,7 @@
 def block_sharded(grad_slab, saved_in, saved_pre, w_proj, w_conv, gain_vec, bias_vec):
     norm_state = norm_forward(saved_pre, gain_vec, bias_vec)
     act_bf = norm_state[5]
-    grad_piece = lax.all_gather(grad_slab, "chan", axis=1, tiled=True)
+    grad_piece = obtain_the_cells(grad_slab)
     fresh = jnp.dot(w_proj, grad_piece, preferred_element_type=jnp.float32)
     weight_acc = lax.dot_general(
         act_bf, grad_piece, (((1,), (1,)), ((), ())), preferred_element_type=jnp.float32

time: 472 us -> 897 us (1.90)
  waiting for transfers between devices: 77.5 us -> 656 us
  blocking collectives: 175 us -> 23.8 us
  other arithmetic: 25.2 us -> 13.1 us
    ppermute x0 -> x120, waiting for transfers between devices: none -> 528 us  [_direct_map(): piece_next = jax.lax.ppermute(piece_next, chip_axis, part_next)]
    all_gather x8 -> x0, blocking collectives: 152 us -> none  [block_sharded(): grad_piece = lax.all_gather(grad_slab, 'chan', axis=1, tiled=True)]
    all_to_all x8, waiting for transfers between devices: 4.02 us -> 59.3 us  [block_sharded(): lax.all_to_all(branch, 'chan', split_axis=1, concat_axis=0, tiled=True)]
    while x232 -> x552, local copies, waits for them, and re-layouts: 4.38 us -> 20.8 us
    dot_general x8, matrix products: 2.62 us -> 12.5 us  [block_sharded(): lax.dot_general(act_bf, grad_piece, (((1,), (1,)), ((), ())), preferred_e...]
  transfers between devices with their start and end apart: 13 -> 133, of which waited for: 9 -> 133; matrix products, arithmetic and copies ran while one was open for 13% -> 5% of each run, Pallas kernels for 0% -> 0%
where the time goes in v1:
time: 897 us; the launch traced here: 894 us
  waiting for transfers between devices  656 us (73%)
  matrix products  69.7 us (8%)
  local copies, waits for them, and re-layouts  63.1 us (7%)
  starting transfers between devices  50 us (6%)
  blocking collectives  23.8 us (3%)
  between operations  14.1 us (2%)
  other arithmetic  13.1 us (1%)
    ppermute x120, waiting for transfers between devices, _direct_map(): piece_next = jax.lax.ppermute(piece_next, chip_axis, part_next)  528 us
    psum x1, waiting for transfers between devices, per_device(): lax.psum((final[2], final[3], final[4], final[5]), 'dp')  61 us
    all_to_all x8, waiting for transfers between devices, block_sharded(): lax.all_to_all(branch, 'chan', split_axis=1, concat_axis=0, tiled=True)  59.3 us
    dot_general x72, matrix products, conv_backward(): jnp.einsum('gop,gjp->goj', grad_pre, source, preferred_element_type=jnp.f...  36.5 us
    all_to_all x8, starting transfers between devices, block_sharded(): lax.all_to_all(branch, 'chan', split_axis=1, concat_axis=0, tiled=True)  32.1 us
    psum x1, blocking collectives, per_device(): lax.psum((final[2], final[3], final[4], final[5]), 'dp')  23.8 us
    while x552, local copies, waits for them, and re-layouts  20.8 us
  transfers between devices with their start and end apart: 133, of which 133 were waited for; matrix products, arithmetic and copies ran while one was open for 5% of the time, Pallas kernels for 0%

profile of v1, /device:TPU:2, one launch (start us, length us, event | category | flops | bytes accessed | tf_op | source)
XLA Modules:
  0.0 894.1 jit_solution(14802116649912672390)
XLA Ops:
  9.6 788.5 %while.26 = (s32[]{:T(128)}, bf16[1536,16]{0,1:T(8,128)(2,1)S(1)}, bf16[1,1,1536,16]{2,3,1,0:T(8,128)(2,1)}, f32[2,96,1536]{2,1,0:T(8,128)S(1)}, f32[2,96,432]{1...) while((s32[]{:T(128)}, bf16[1536,16]{0,1:T(8,128)(2,1)S(1)}, ...), condition=%wide.region_21.23_spmd.clone, body=%wide.region_0.22_spmd.clone.sunk | while | flops 399012256 | bytes 46313544 | solution.py:176
  10.5 4.7 collective-permute-done
  15.2 4.7 collective-permute-done.1
  19.9 4.7 collective-permute-done.2
  24.6 4.7 collective-permute-done.3
  34.3 4.6 collective-permute-done.5
  43.7 4.6 collective-permute-done.7
  53.0 4.7 collective-permute-done.9
  67.2 4.7 collective-permute-done.12
  71.9 4.7 collective-permute-done.13
  85.7 7.3 all-to-all-start
  93.1 7.7 all-to-all-done
  110.7 4.6 collective-permute-done.17
  143.8 4.6 collective-permute-done.24
  148.6 4.5 collective-permute-done.25
  153.3 4.5 collective-permute-done.26
  158.1 4.5 collective-permute-done.27
  162.8 4.6 collective-permute-done.28
  196.2 7.2 all-to-all-done.1
  210.5 4.7 collective-permute-done
  215.2 4.7 collective-permute-done.1
  219.9 4.7 collective-permute-done.2
  224.7 4.7 collective-permute-done.3
  234.3 4.6 collective-permute-done.5
  243.7 4.6 collective-permute-done.7
  253.0 4.7 collective-permute-done.9
  267.2 4.7 collective-permute-done.12
  271.9 4.7 collective-permute-done.13
  289.4 7.6 all-to-all-done
  306.9 4.6 collective-permute-done.17
  340.0 4.6 collective-permute-done.24
  344.8 4.5 collective-permute-done.25
  359.0 4.6 collective-permute-done.28
  392.4 7.2 all-to-all-done.1
  406.7 4.7 collective-permute-done
  411.4 4.7 collective-permute-done.1
  416.1 4.7 collective-permute-done.2
  420.8 4.7 collective-permute-done.3
  430.5 4.6 collective-permute-done.5
  439.9 4.6 collective-permute-done.7
  449.2 4.7 collective-permute-done.9
  463.4 4.7 collective-permute-done.12
  468.1 4.7 collective-permute-done.13
  485.6 7.6 all-to-all-done
  503.1 4.6 collective-permute-done.17
  536.2 4.6 collective-permute-done.24
  555.2 4.6 collective-permute-done.28
  588.6 7.2 all-to-all-done.1
  602.9 4.7 collective-permute-done
  607.6 4.7 collective-permute-done.1
  612.3 4.7 collective-permute-done.2
  617.0 4.7 collective-permute-done.3
  626.6 4.6 collective-permute-done.5
  636.1 4.6 collective-permute-done.7
  645.4 4.7 collective-permute-done.9
  659.6 4.7 collective-permute-done.12
  664.3 4.7 collective-permute-done.13
  681.8 7.6 all-to-all-done
  699.3 4.6 collective-permute-done.17
  732.4 4.6 collective-permute-done.24
  751.3 4.6 collective-permute-done.28
  784.8 7.2 all-to-all-done.1
  799.3 23.8 %all-reduce.18 = (f32[1,2,96]{2,1,0:T(2,128)}, f32[1,2,96]{2,1,0:T(2,128)}) all-reduce(f32[1,2,96]{2,1,0:T(2,128)S(1)} %bitcast.574, f32[1,2,96]{2,1,0:T(2,128)S(1)} %bitcast.575), channel_id=1, replica_groups=mesh['segment'=4,'chan'=16,'dp'=8] {'dp'}, use_global_device_ids=true, to_apply=%region_24.26 | all-reduce | flops 384 | bytes 3072 | tf_op jit(solution)/shard_map/psum | solution.py:178
  823.1 61.0 %all-reduce.22.cloned.1.call-done = (f32[1,2,96,1536]{3,2,1,0:T(8,128)}, f32[1,2,96,432]{3,2,1,0:T(8,128)}) async-done(((f32[1,2,96,1536]{3,2,1,0:T(8,128)}, f32[1,2,96,432]{3,2,1,0:T(8,128)}), (f32[1,2,96,1536]{3,2,1,0:T(8,128)}, f32[1,2,96,432]{3,2,1,0:T(8,128)})) %all-reduce.22.cloned.1.call-update) | async-done | bytes 1511440 | tf_op jit(solution)/shard_map/psum | solution.py:178
  (1227 shorter events, 482.5 us)
Async XLA Ops:
  7.2 876.9 %all-reduce.22.cloned.1.call-start = ((), (), s32[]{:S(2)}) async-start(), calls=%async_computation.2 | async-start | bytes 3145728 | tf_op jit(solution)/shard_map/psum | solution.py:178
  19.9 4.7 collective-permute-start.2
  24.6 4.7 collective-permute-start.3
  43.5 4.7 collective-permute-start.7
  48.3 4.7 collective-permute-start.8
  67.2 4.7 collective-permute-start.12
  71.9 4.7 collective-permute-start.13
  85.7 15.2 %all-to-all-start = ((bf16[96,16,16]{0,2,1:T(8,128)(2,1)}), bf16[96,16,16]{0,2,1:T(8,128)(2,1)S(1)}, u32[]{:S(2)}, u32[]{:S(2)}) async-start(bf16[96,16,16]{0,2,1:T(8,128)(2,1)} %convert_element_type.430), calls=%async_computation | async-start | bytes 131072 | tf_op jit(solution)/shard_map/while/body/eval_jaxpr/all_to_all | solution.py:105
  101.1 4.7 collective-permute-start.15
  110.6 4.7 collective-permute-start.17
  115.3 4.7 collective-permute-start.18
  134.2 4.7 collective-permute-start.22
  138.9 4.7 collective-permute-start.23
  143.7 4.7 collective-permute-start.24
  148.4 4.7 collective-permute-start.25
  153.1 4.7 collective-permute-start.26
  157.8 4.7 collective-permute-start.27
  162.6 4.8 collective-permute-start.28
  167.5 5.1 collective-permute-start.29
  192.1 11.3 %all-to-all-start.1 = ((bf16[96,16,16]{0,2,1:T(8,128)(2,1)}), bf16[96,16,16]{0,2,1:T(8,128)(2,1)S(1)}, u32[]{:S(2)}, u32[]{:S(2)}) async-start(bf16[96,16,16]{0,2,1:T(8,128)(2,1)} %convert_element_type.431), calls=%async_computation.1 | async-start | bytes 131072 | tf_op jit(solution)/shard_map/while/body/eval_jaxpr/all_to_all | solution.py:105
  203.6 6.0 collective-permute-start.30
  219.9 4.7 collective-permute-start.2
  224.7 4.7 collective-permute-start.3
  238.8 4.7 collective-permute-start.6
  243.6 4.7 collective-permute-start.7
  248.3 4.7 collective-permute-start.8
  262.5 4.7 collective-permute-start.11
  267.2 4.7 collective-permute-start.12
  285.7 11.4 %all-to-all-start = ((bf16[96,16,16]{0,2,1:T(8,128)(2,1)}), bf16[96,16,16]{0,2,1:T(8,128)(2,1)S(1)}, u32[]{:S(2)}, u32[]{:S(2)}) async-start(bf16[96,16,16]{0,2,1:T(8,128)(2,1)} %convert_element_type.430), calls=%async_computation | async-start | bytes 131072 | tf_op jit(solution)/shard_map/while/body/eval_jaxpr/all_to_all | solution.py:105
  297.3 4.7 collective-permute-start.15
  311.5 4.7 collective-permute-start.18
  316.2 4.7 collective-permute-start.19
  320.9 4.7 collective-permute-start.20
  325.7 4.7 collective-permute-start.21
  330.4 4.7 collective-permute-start.22
  335.1 4.7 collective-permute-start.23
  358.8 4.8 collective-permute-start.28
  363.7 5.1 collective-permute-start.29
  388.3 11.3 %all-to-all-start.1 = ((bf16[96,16,16]{0,2,1:T(8,128)(2,1)}), bf16[96,16,16]{0,2,1:T(8,128)(2,1)S(1)}, u32[]{:S(2)}, u32[]{:S(2)}) async-start(bf16[96,16,16]{0,2,1:T(8,128)(2,1)} %convert_element_type.431), calls=%async_computation.1 | async-start | bytes 131072 | tf_op jit(solution)/shard_map/while/body/eval_jaxpr/all_to_all | solution.py:105
  399.8 6.0 collective-permute-start.30
  406.7 4.7 collective-permute-start
  425.6 4.7 collective-permute-start.4
  430.3 4.7 collective-permute-start.5
  444.5 4.7 collective-permute-start.8
  449.2 4.7 collective-permute-start.9
  453.9 4.7 collective-permute-start.10
  468.1 4.7 collective-permute-start.13
  472.8 4.7 collective-permute-start.14
  481.9 11.4 %all-to-all-start = ((bf16[96,16,16]{0,2,1:T(8,128)(2,1)}), bf16[96,16,16]{0,2,1:T(8,128)(2,1)S(1)}, u32[]{:S(2)}, u32[]{:S(2)}) async-start(bf16[96,16,16]{0,2,1:T(8,128)(2,1)} %convert_element_type.430), calls=%async_computation | async-start | bytes 131072 | tf_op jit(solution)/shard_map/while/body/eval_jaxpr/all_to_all | solution.py:105
  493.5 4.7 collective-permute-start.15
  512.4 4.7 collective-permute-start.19
  517.1 4.7 collective-permute-start.20
  521.9 4.7 collective-permute-start.21
  555.0 4.8 collective-permute-start.28
  559.9 5.1 collective-permute-start.29
  584.5 11.3 %all-to-all-start.1 = ((bf16[96,16,16]{0,2,1:T(8,128)(2,1)}), bf16[96,16,16]{0,2,1:T(8,128)(2,1)S(1)}, u32[]{:S(2)}, u32[]{:S(2)}) async-start(bf16[96,16,16]{0,2,1:T(8,128)(2,1)} %convert_element_type.431), calls=%async_computation.1 | async-start | bytes 131072 | tf_op jit(solution)/shard_map/while/body/eval_jaxpr/all_to_all | solution.py:105
  596.0 6.0 collective-permute-start.30
  617.0 4.7 collective-permute-start.3
  678.1 11.4 %all-to-all-start = ((bf16[96,16,16]{0,2,1:T(8,128)(2,1)}), bf16[96,16,16]{0,2,1:T(8,128)(2,1)S(1)}, u32[]{:S(2)}, u32[]{:S(2)}) async-start(bf16[96,16,16]{0,2,1:T(8,128)(2,1)} %convert_element_type.430), calls=%async_computation | async-start | bytes 131072 | tf_op jit(solution)/shard_map/while/body/eval_jaxpr/all_to_all | solution.py:105
  689.7 4.7 collective-permute-start.15
  751.1 4.8 collective-permute-start.28
  756.0 5.1 collective-permute-start.29
  780.6 11.3 %all-to-all-start.1 = ((bf16[96,16,16]{0,2,1:T(8,128)(2,1)}), bf16[96,16,16]{0,2,1:T(8,128)(2,1)S(1)}, u32[]{:S(2)}, u32[]{:S(2)}) async-start(bf16[96,16,16]{0,2,1:T(8,128)(2,1)} %convert_element_type.431), calls=%async_computation.1 | async-start | bytes 131072 | tf_op jit(solution)/shard_map/while/body/eval_jaxpr/all_to_all | solution.py:105
  792.1 6.0 collective-permute-start.30
  (289 other events, 3933.2 us)
Sparse Core Ops, SparseCore 0:
  799.5 84.6 all-reduce.21
